TPU v7x, 32 devices: a whole 2x2x4 slice. The times are simulated.
32 devices in a mesh: groups: 2 (over y), cells: 4 (over z), corners: 2 (over x), kern: 2 (over core).
Axes of the slice: x: 2, y: 2, z: 4, core: 2. Of those that a mesh axis runs over, the one named last changes fastest.
Arguments:
- theta: float32 [64, 128, 128], P(('groups', 'cells')), parts along dimension 0, may hold values from -8 to 8
- target: bfloat16 [16, 128, 128], P(('groups', 'cells')), parts along dimension 0, may hold values from 0 to 1
- kernels: float32 [2, 2, 24, 35, 35], P(None, 'corners', 'kern'), may hold values from -25.33743 to 25.33743
- dose: float32 [2], P('corners'), may hold values from 0.6 to 1
- inst_owner: int32 [128, 1], P(('groups', 'cells')), parts along dimension 0, may hold values from 0 to 3; in each aligned block of 16 rows (0 to 15, 16 to 31, ...) at most 8 rows name the same one
- inst_local: int32 [128], P(('groups', 'cells')), parts along dimension 0, may hold values from 0 to 7
- inst_shift: int32 [128], P(('groups', 'cells')), parts along dimension 0, may hold values from 0 to 127
Outputs:
- theta_out: float32 [64, 128, 128], P(('groups', 'cells'), ('corners', 'kern')), parts along dimension 0
There are 2 independent parts, one for each index of `groups`. A program takes and returns all parts, laid end to end along the dimension named above; an argument that names none is the same for every part. Nothing has to cross between parts.
Inputs may be any that keep to these rules, and one draw needn't show every extreme that they name: `inst_owner`: within the rows of one device (aligned blocks of 16 rows) no owner is named by more than 8 rows, and in some block one owner is named by exactly 8.
All inputs are finite; a program needn't handle non-finite values.
Results may differ from a plain program's by a relative error of at most 0.003.
Values may be sent and summed in bfloat16 or wider, within the bound.
No kernel may reach another device: no remote copies, remote signals or barrier semaphores. Data moves between devices by JAX's collectives and lax.ppermute only.
A program may use at most 64 MiB of HBM per device.

v0:
```python
import math
import jax
import jax.numpy as jnp
from jax import lax
from jax.sharding import PartitionSpec as P

ITERS = 2
LR = 0.25
EPS = 1e-06
STEEP = 3.0


def tables(cell_size, freq_count):
    freqs = jnp.arange(freq_count, dtype=jnp.int32) - freq_count // 2
    pixels = jnp.arange(cell_size, dtype=jnp.int32)
    phase = (freqs[:, None] * pixels[None, :] % cell_size).astype(jnp.float32) * (
        2.0 * math.pi / cell_size
    )
    fwd_real = jnp.cos(phase)
    fwd_imag = -jnp.sin(phase)
    inv_real = fwd_real.T / cell_size
    inv_imag = -fwd_imag.T / cell_size
    return (fwd_real, fwd_imag, inv_real, inv_imag)


def spectrum(field, tabs):
    fwd_real, fwd_imag = (tabs[0], tabs[1])
    hp = lax.Precision.HIGHEST
    left_real = jnp.einsum("fx,txy->tfy", fwd_real, field, precision=hp)
    left_imag = jnp.einsum("fx,txy->tfy", fwd_imag, field, precision=hp)
    spec_real = jnp.einsum("tfy,gy->tfg", left_real, fwd_real, precision=hp) - jnp.einsum(
        "tfy,gy->tfg", left_imag, fwd_imag, precision=hp
    )
    spec_imag = jnp.einsum("tfy,gy->tfg", left_real, fwd_imag, precision=hp) + jnp.einsum(
        "tfy,gy->tfg", left_imag, fwd_real, precision=hp
    )
    return (spec_real, spec_imag)


def intensity(field, kern_real, kern_imag, tabs):
    inv_real, inv_imag = (tabs[2], tabs[3])
    hp = lax.Precision.HIGHEST
    spec_real, spec_imag = spectrum(field, tabs)

    def add_kernel(running, pair):
        resp_real = pair[0] * spec_real - pair[1] * spec_imag
        resp_imag = pair[0] * spec_imag + pair[1] * spec_real
        half_real = jnp.einsum("tfg,yg->tfy", resp_real, inv_real, precision=hp) - jnp.einsum(
            "tfg,yg->tfy", resp_imag, inv_imag, precision=hp
        )
        half_imag = jnp.einsum("tfg,yg->tfy", resp_real, inv_imag, precision=hp) + jnp.einsum(
            "tfg,yg->tfy", resp_imag, inv_real, precision=hp
        )
        near_real = jnp.einsum("xf,tfy->txy", inv_real, half_real, precision=hp) - jnp.einsum(
            "xf,tfy->txy", inv_imag, half_imag, precision=hp
        )
        near_imag = jnp.einsum("xf,tfy->txy", inv_real, half_imag, precision=hp) + jnp.einsum(
            "xf,tfy->txy", inv_imag, half_real, precision=hp
        )
        return (running + near_real * near_real + near_imag * near_imag, None)

    start = jnp.zeros(field.shape, jnp.float32)
    result, unused = lax.scan(add_kernel, start, (kern_real, kern_imag))
    return result


def per_device(theta, target, kernels, dose, inst_owner, inst_local, inst_shift):
    hp = lax.Precision.HIGHEST
    n_owners = lax.axis_size("cells")
    members = lax.axis_size(("corners", "kern"))
    member = lax.axis_index(("corners", "kern"))
    cells_here = theta.shape[0]
    cell_size = theta.shape[1]
    inst_count = inst_local.shape[0]
    tile_count = target.shape[0]
    slot_count = inst_count // tile_count
    capacity = max(2, 2 * inst_count // n_owners)
    band_rows = cell_size // members
    tabs = tables(cell_size, kernels.shape[3])
    dose_now = dose[0]
    wanted = target.astype(jnp.float32)
    kern_real = kernels[0, 0]
    kern_imag = kernels[1, 0]
    owners = inst_owner[:, 0]
    inst_iota = jnp.arange(inst_count, dtype=jnp.int32)
    same_owner = (owners[None, :] == owners[:, None]) & (inst_iota[None, :] < inst_iota[:, None])
    rank_in = jnp.sum(same_owner.astype(jnp.int32), axis=1)
    slot_index = owners * capacity + rank_in
    slot_hit = slot_index[:, None] == jnp.arange(n_owners * capacity, dtype=jnp.int32)[None, :]
    used_slot = jnp.any(slot_hit, axis=0)
    asked_local = jnp.sum(jnp.where(slot_hit, inst_local[:, None], 0), axis=0)
    request = jnp.where(used_slot, asked_local, -1).reshape(n_owners, capacity)
    asked = lax.all_to_all(request, "cells", split_axis=0, concat_axis=0, tiled=True)
    picker = (
        asked.reshape(-1)[:, None] == jnp.arange(cells_here, dtype=jnp.int32)[None, :]
    ).astype(jnp.float32)
    picker_half = picker.astype(jnp.bfloat16)
    slot_weights = slot_hit.astype(jnp.float32)
    cell_params = lax.dynamic_slice_in_dim(theta, member * band_rows, band_rows, 1)
    rows_here = cell_params.shape[1]
    for iteration in range(ITERS):
        mask_vals = jax.nn.sigmoid(cell_params).astype(jnp.bfloat16)
        outgoing = jnp.dot(
            picker_half, mask_vals.reshape(cells_here, -1), preferred_element_type=jnp.float32
        )
        outgoing = outgoing.astype(jnp.bfloat16).reshape(n_owners, capacity, rows_here, cell_size)
        received = lax.all_to_all(outgoing, "cells", split_axis=0, concat_axis=0, tiled=True)
        placed = jnp.take(
            received.reshape(n_owners * capacity, rows_here, cell_size), slot_index, axis=0
        )
        transmit = 2.0 * placed.astype(jnp.float32) - 1.0
        rolled = jax.vmap(lambda plane, offset: jnp.roll(plane, offset, axis=1))(
            transmit, inst_shift
        )
        tile_part = (
            jnp.sum(rolled.reshape(tile_count, slot_count, rows_here, cell_size), axis=1)
            / slot_count
        )
        tile_field = lax.all_gather(tile_part, ("corners", "kern"), axis=1, tiled=True)
        partial_image, pullback = jax.vjp(
            lambda plane: intensity(plane, kern_real, kern_imag, tabs), tile_field
        )
        image = lax.psum(partial_image.astype(jnp.bfloat16), "kern").astype(jnp.float32)
        resist = jax.nn.sigmoid(STEEP * (dose_now * image - 1.0))
        pressure = 2.0 * (resist - wanted) * resist * (1.0 - resist) * STEEP * dose_now
        tile_grad = pullback(pressure)[0]
        grad_part = lax.psum_scatter(
            tile_grad.astype(jnp.bfloat16), ("corners", "kern"), scatter_dimension=1, tiled=True
        ).astype(jnp.float32)
        inst_grads = jnp.repeat(grad_part, slot_count, axis=0)
        unrolled = jax.vmap(lambda plane, offset: jnp.roll(plane, -offset, axis=1))(
            inst_grads, inst_shift
        )
        slot_grads = jnp.dot(slot_weights.T, unrolled.reshape(inst_count, -1), precision=hp)
        slot_grads = slot_grads.reshape(n_owners, capacity, rows_here, cell_size)
        returned = lax.all_to_all(slot_grads, "cells", split_axis=0, concat_axis=0, tiled=True)
        cell_sums = jnp.dot(picker.T, returned.reshape(n_owners * capacity, -1), precision=hp)
        cell_sums = cell_sums.reshape(cells_here, rows_here, cell_size)
        squash = jax.nn.sigmoid(cell_params)
        gradient = cell_sums * (2.0 / slot_count) * squash * (1.0 - squash)
        squares = jnp.sum(gradient * gradient, axis=(1, 2))
        squares = lax.psum(squares, ("corners", "kern"))
        cell_params = (
            cell_params
            - LR * gradient / jnp.sqrt(squares / (cell_size * cell_size) + EPS)[:, None, None]
        )
    return cell_params


def solution(mesh):
    in_specs = (
        P(("groups", "cells"), None, None),
        P(("groups", "cells"), None, None),
        P(None, "corners", "kern", None, None),
        P("corners"),
        P(("groups", "cells"), None),
        P(("groups", "cells")),
        P(("groups", "cells")),
    )
    out_specs = P(("groups", "cells"), ("corners", "kern"), None)
    return jax.shard_map(
        per_device, mesh=mesh, in_specs=in_specs, out_specs=out_specs, check_vma=False
    )
```

profile of v0, /device:TPU:0, one launch (start us, length us, event | category | flops | bytes accessed | tf_op | source)
XLA Modules:
  0.0 497.6 jit_solution(15146863222986831006)
XLA Ops:
  9.6 6.3 %all-to-all-start = ((s32[4,1,8]{2,1,0:T(1,128)}), s32[4,1,8]{2,1,0:T(1,128)S(1)}, u32[]{:S(2)}, u32[]{:S(2)}) async-start(s32[4,1,8]{2,1,0:T(1,128)} %bitcast.3), calls=%async_computation | async-start | bytes 4096 | tf_op jit(solution)/shard_map/all_to_all | solution.py:93
  18.4 3.1 all-to-all-done
  23.7 3.4 all-to-all-start.1
  28.0 6.2 %all-to-all-done.1 = bf16[4,8,32,128]{3,2,1,0:T(8,128)(2,1)S(1)} async-done(((bf16[4,8,32,128]{3,2,1,0:T(8,128)(2,1)}), bf16[4,8,32,128]{3,2,1,0:T(8,128)(2,1)S(1)}, u32[]{:S(2)}, u32[]{:S(2)}) %all-to-all-start.1) | async-done | bytes 262176 | tf_op jit(solution)/shard_map/all_to_all | solution.py:107
  34.9 1.3 copy.84
  36.2 3.0 gather_fusion.1
  39.2 1.6 bitcast_reduce_fusion.1
  40.9 5.4 %all_gather.6 = f32[2,128,128]{2,1,0:T(8,128)S(1)} all-gather(f32[2,32,128]{2,1,0:T(8,128)S(1)} %broadcast_multiply_fusion.1), channel_id=1, replica_groups=mesh['groups'=2,'cells'=4,'corners'=2,'kern'=2] {'corners','kern'}, dimensions={1}, use_global_device_ids=true | all-gather | bytes 163840 | tf_op jit(solution)/shard_map/all_gather | solution.py:119
  48.3 1.3 broadcast.159.clone
  49.9 63.0 %while.92 = (s32[]{:T(128)}, f32[2,128,128]{1,2,0:T(8,128)S(1)}, f32[12,1,35,35]{3,2,1,0:T(8,128)S(1)}, f32[12,1,35,35]{3,2,1,0:T(8,128)S(1)}, f32[12,2,128,128]...) while((s32[]{:T(128)}, f32[2,128,128]{1,2,0:T(8,128)S(1)}, ...), condition=%wide.region_5.8_spmd.clone.clone.clone.clone, body=%wide.region_4.7_spmd.clone.clone.clone.clone.sunk | while | flops 70917336 | bytes 2136583 | solution.py:63
  114.6 16.4 %all-reduce.8.cloned.1.call-done = bf16[2,128,128]{1,2,0:T(8,128)(2,1)} async-done(((bf16[2,128,128]{1,2,0:T(8,128)(2,1)}), bf16[2,128,128]{1,2,0:T(8,128)(2,1)}) %all-reduce.8.cloned.1.call-update) | async-done | bytes 65552 | tf_op jit(solution)/shard_map/psum | solution.py:123
  132.0 56.9 %while.93 = (s32[]{:T(128)}, f32[2,35,35]{2,1,0:T(8,128)S(1)}, f32[2,35,35]{2,1,0:T(8,128)S(1)}, f32[12,1,35,35]{3,2,1,0:T(8,128)S(1)}, f32[12,2,128,128]{2,3,1,...) while((s32[]{:T(128)}, f32[2,35,35]{2,1,0:T(8,128)S(1)}, ...), condition=%wide.region_8.11_spmd.clone.clone.clone.clone, body=%wide.region_7.10_spmd.clone.clone.clone.clone.sunk | while | flops 70994280 | bytes 1536399 | solution.py:63
  139.1 1.3 fusion.694
  143.9 1.3 fusion.694
  148.6 1.3 fusion.694
  153.4 1.3 fusion.694
  158.1 1.3 fusion.694
  162.8 1.3 fusion.694
  167.6 1.3 fusion.694
  172.3 1.3 fusion.694
  177.1 1.3 fusion.694
  181.8 1.3 fusion.694
  186.5 1.3 fusion.694
  193.2 31.6 %all-reduce.12.cloned.1.call-done = bf16[2,128,128]{2,0,1:T(2,128)(2,1)} async-done(((bf16[2,128,128]{2,0,1:T(2,128)(2,1)}), bf16[2,128,128]{2,0,1:T(2,128)(2,1)}) %all-reduce.12.cloned.1.call-update) | async-done | bytes 65552
  225.5 1.3 copy.90
  226.8 3.0 gather_fusion.2
  229.8 1.6 copy.91
  232.0 17.8 %all_to_all.26 = f32[4,8,32,128]{3,1,2,0:T(8,128)S(1)} all-to-all(f32[4,8,32,128]{3,1,2,0:T(8,128)S(1)} %fusion.356), channel_id=1, replica_groups=mesh['groups'=2,'cells'=4,'corners'=2,'kern'=2] {'cells'}, dimensions={0} | all-to-all | bytes 1048576 | tf_op jit(solution)/shard_map/all_to_all | solution.py:136
  250.2 5.7 %psum.29 = f32[8]{0:T(128)S(1)} all-reduce(f32[8]{0:T(128)S(1)} %get-tuple-element.1373), channel_id=1, replica_groups=mesh['groups'=2,'cells'=4,'corners'=2,'kern'=2] {'corners','kern'}, use_global_device_ids=true, to_apply=%region_11.14 | all-reduce | flops 8 | bytes 64 | tf_op jit(solution)/shard_map/psum | solution.py:142
  257.0 3.4 all-to-all-start.3
  260.5 9.1 %all-to-all-done.3 = bf16[4,8,32,128]{3,2,1,0:T(8,128)(2,1)S(1)} async-done(((bf16[4,8,32,128]{3,2,1,0:T(8,128)(2,1)}), bf16[4,8,32,128]{3,2,1,0:T(8,128)(2,1)S(1)}, u32[]{:S(2)}, u32[]{:S(2)}) %all-to-all-start.3) | async-done | bytes 262176 | tf_op jit(solution)/shard_map/all_to_all | solution.py:107
  270.4 1.3 copy.95
  271.7 3.0 gather_fusion.4
  274.7 1.6 bitcast_reduce_fusion
  276.3 5.6 %all_gather.7 = f32[2,128,128]{2,1,0:T(8,128)S(1)} all-gather(f32[2,32,128]{2,1,0:T(8,128)S(1)} %broadcast_multiply_fusion), channel_id=1, replica_groups=mesh['groups'=2,'cells'=4,'corners'=2,'kern'=2] {'corners','kern'}, dimensions={1}, use_global_device_ids=true | all-gather | bytes 163840 | tf_op jit(solution)/shard_map/all_gather | solution.py:119
  284.0 1.3 broadcast.159
  285.5 63.0 %while.94 = (s32[]{:T(128)}, f32[2,128,128]{1,2,0:T(8,128)S(1)}, f32[12,1,35,35]{3,2,1,0:T(8,128)S(1)}, f32[12,1,35,35]{3,2,1,0:T(8,128)S(1)}, f32[12,2,128,128]...) while((s32[]{:T(128)}, f32[2,128,128]{1,2,0:T(8,128)S(1)}, ...), condition=%wide.region_14.17_spmd.clone.clone.clone.clone, body=%wide.region_13.16_spmd.clone.clone.clone.clone.sunk | while | flops 70917336 | bytes 2136583 | solution.py:63
  349.3 16.2 %all-reduce.10.cloned.1.call-done = bf16[2,128,128]{1,2,0:T(8,128)(2,1)} async-done(((bf16[2,128,128]{1,2,0:T(8,128)(2,1)}), bf16[2,128,128]{1,2,0:T(8,128)(2,1)}) %all-reduce.10.cloned.1.call-update) | async-done | bytes 65552 | tf_op jit(solution)/shard_map/psum | solution.py:123
  366.4 56.9 %while.95 = (s32[]{:T(128)}, f32[2,35,35]{2,1,0:T(8,128)S(1)}, f32[2,35,35]{2,1,0:T(8,128)S(1)}, f32[12,1,35,35]{3,2,1,0:T(8,128)S(1)}, f32[12,2,128,128]{2,3,1,...) while((s32[]{:T(128)}, f32[2,35,35]{2,1,0:T(8,128)S(1)}, ...), condition=%wide.region_17.20_spmd.clone.clone.clone.clone, body=%wide.region_16.19_spmd.clone.clone.clone.clone.sunk | while | flops 70994280 | bytes 1536399 | solution.py:63
  373.5 1.3 fusion.731
  378.3 1.3 fusion.731
  411.5 1.3 fusion.731
  426.3 32.9 %all-reduce.14.cloned.1.call-done = bf16[2,128,128]{2,0,1:T(2,128)(2,1)} async-done(((bf16[2,128,128]{2,0,1:T(2,128)(2,1)}), bf16[2,128,128]{2,0,1:T(2,128)(2,1)}) %all-reduce.14.cloned.1.call-update) | async-done | bytes 65552
  460.0 1.3 copy.99
  461.3 3.0 gather_fusion.5
  464.3 1.6 copy.100
  466.4 17.8 %all_to_all.27 = f32[4,8,32,128]{3,1,2,0:T(8,128)S(1)} all-to-all(f32[4,8,32,128]{3,1,2,0:T(8,128)S(1)} %fusion.354), channel_id=1, replica_groups=mesh['groups'=2,'cells'=4,'corners'=2,'kern'=2] {'cells'}, dimensions={0} | all-to-all | bytes 1048576 | tf_op jit(solution)/shard_map/all_to_all | solution.py:136
  484.6 5.7 %psum.31 = f32[8]{0:T(128)S(1)} all-reduce(f32[8]{0:T(128)S(1)} %get-tuple-element.1375), channel_id=1, replica_groups=mesh['groups'=2,'cells'=4,'corners'=2,'kern'=2] {'corners','kern'}, use_global_device_ids=true, to_apply=%region_20.23 | all-reduce | flops 8 | bytes 64 | tf_op jit(solution)/shard_map/psum | solution.py:142
  (584 shorter events, 247.7 us)
Async XLA Ops:
  6.5 11.9 %copy-start = (f32[8,128,128]{2,1,0:T(8,128)S(1)}, f32[8,128,128]{2,1,0:T(8,128)}, u32[]{:S(2)}) copy-start(f32[8,128,128]{2,1,0:T(8,128)} %param.19) | copy-start | bytes 1572868
  9.6 11.9 %all-to-all-start = ((s32[4,1,8]{2,1,0:T(1,128)}), s32[4,1,8]{2,1,0:T(1,128)S(1)}, u32[]{:S(2)}, u32[]{:S(2)}) async-start(s32[4,1,8]{2,1,0:T(1,128)} %bitcast.3), calls=%async_computation | async-start | bytes 4096 | tf_op jit(solution)/shard_map/all_to_all | solution.py:93
  18.4 8.8 %copy-start.3 = (f32[8,32,128]{2,1,0:T(8,128)}, f32[8,32,128]{2,1,0:T(8,128)S(1)}, u32[]{:S(2)}) copy-start(f32[8,32,128]{2,1,0:T(8,128)S(1)} %constant_dynamic-slice_fusion.2) | copy-start | bytes 393220
  23.7 10.5 %all-to-all-start.1 = ((bf16[4,8,32,128]{3,2,1,0:T(8,128)(2,1)}), bf16[4,8,32,128]{3,2,1,0:T(8,128)(2,1)S(1)}, u32[]{:S(2)}, u32[]{:S(2)}) async-start(bf16[4,8,32,128]{3,2,1,0:T(8,128)(2,1)} %copy.83), calls=%async_computation.1 | async-start | bytes 524288 | tf_op jit(solution)/shard_map/all_to_all | solution.py:107
  27.1 103.9 %all-reduce.8.cloned.1.call-start = ((), (), s32[]{:S(2)}) async-start(), calls=%async_computation.5 | async-start | bytes 131072 | tf_op jit(solution)/shard_map/psum | solution.py:123
  49.9 64.6 %copy-start.7 = (bf16[2,128,128]{2,1,0:T(8,128)(2,1)S(1)}, bf16[2,128,128]{2,1,0:T(8,128)(2,1)}, u32[]{:S(2)}) copy-start(bf16[2,128,128]{2,1,0:T(8,128)(2,1)} %param.20) | copy-start | bytes 196612
  113.6 111.2 %all-reduce.12.cloned.1.call-start = ((), (), s32[]{:S(2)}) async-start(), calls=%async_computation.7 | async-start | bytes 131072
  114.6 17.4 %copy-start.1 = (bf16[2,128,128]{1,2,0:T(8,128)(2,1)}, bf16[2,128,128]{1,2,0:T(8,128)(2,1)S(1)}, u32[]{:S(2)}) copy-start(bf16[2,128,128]{1,2,0:T(8,128)(2,1)S(1)} %copy.87) | copy-start | bytes 196612
  131.9 59.9 %copy-start.8 = (u32[32]{0:T(128)S(1)}, u32[32]{0:T(128)}, u32[]{:S(2)}) copy-start(u32[32]{0:T(128)} %constant.353) | copy-start | bytes 388
  229.8 19.9 %copy-start.4 = (f32[8,32,128]{2,1,0:T(8,128)S(1)}, f32[8,32,128]{2,1,0:T(8,128)}, u32[]{:S(2)}) copy-start(f32[8,32,128]{2,1,0:T(8,128)} %copy-done.3) | copy-start | bytes 393220
  256.0 14.3 %copy-start.5 = (f32[8,32,128]{2,0,1:T(8,128)}, f32[8,32,128]{2,0,1:T(8,128)S(1)}, u32[]{:S(2)}) copy-start(f32[8,32,128]{2,0,1:T(8,128)S(1)} %divide_subtract_fusion.1) | copy-start | bytes 393220
  257.0 12.6 %all-to-all-start.3 = ((bf16[4,8,32,128]{3,2,1,0:T(8,128)(2,1)}), bf16[4,8,32,128]{3,2,1,0:T(8,128)(2,1)S(1)}, u32[]{:S(2)}, u32[]{:S(2)}) async-start(bf16[4,8,32,128]{3,2,1,0:T(8,128)(2,1)} %copy.94), calls=%async_computation.3 | async-start | bytes 524288 | tf_op jit(solution)/shard_map/all_to_all | solution.py:107
  260.4 105.0 %all-reduce.10.cloned.1.call-start = ((), (), s32[]{:S(2)}) async-start(), calls=%async_computation.6 | async-start | bytes 131072 | tf_op jit(solution)/shard_map/psum | solution.py:123
  285.5 80.0 %copy-start.2 = (bf16[2,128,128]{1,2,0:T(8,128)(2,1)S(1)}, bf16[2,128,128]{1,2,0:T(8,128)(2,1)}, u32[]{:S(2)}) copy-start(bf16[2,128,128]{1,2,0:T(8,128)(2,1)} %copy-done.1) | copy-start | bytes 196612
  349.2 109.9 %all-reduce.14.cloned.1.call-start = ((), (), s32[]{:S(2)}) async-start(), calls=%async_computation.8 | async-start | bytes 131072
  464.3 19.9 %copy-start.6 = (f32[8,32,128]{2,0,1:T(8,128)S(1)}, f32[8,32,128]{2,0,1:T(8,128)}, u32[]{:S(2)}) copy-start(f32[8,32,128]{2,0,1:T(8,128)} %copy-done.5) | copy-start | bytes 393220
Sparse Core Ops, SparseCore 0:
  113.7 17.2 all-reduce.7
  192.0 32.7 all-reduce.11
  349.3 16.0 all-reduce.9
  426.4 32.7 all-reduce.13
where the time goes:
time: 502 us; the launch traced here: 498 us
  matrix products  211 us (42%)
  waiting for transfers between devices  116 us (23%)
  local copies, waits for them, and re-layouts  69.9 us (14%)
  blocking collectives  58 us (12%)
  between operations  15.1 us (3%)
  starting transfers between devices  13.5 us (3%)
  other arithmetic  11.2 us (2%)
    unnamed x6, waiting for transfers between devices  64.5 us
    dot_general x48, matrix products, add_kernel(): jnp.einsum('xf,tfy->txy', inv_imag, half_imag, precision=hp)  57.2 us
    dot_general x48, matrix products, add_kernel(): jnp.einsum('xf,tfy->txy', inv_real, half_real, precision=hp)  41.5 us
    all_to_all x2, blocking collectives, per_device(): lax.all_to_all(slot_grads, 'cells', split_axis=0, concat_axis=0, tiled=True)  35.6 us
    psum x2, waiting for transfers between devices, per_device(): lax.psum(partial_image.astype(jnp.bfloat16), 'kern').astype(jnp.float32)  32.6 us
    dot_general x48, matrix products, add_kernel(): jnp.einsum('xf,tfy->txy', inv_imag, half_real, precision=hp)  19.8 us
    dot_general x48, matrix products, add_kernel(): jnp.einsum('xf,tfy->txy', inv_real, half_imag, precision=hp)  19.5 us
    dynamic_update_slice x48, local copies, waits for them, and re-layouts, intensity(): result, unused = lax.scan(add_kernel, start, (kern_real, kern_imag))  18.1 us
  transfers between devices with their start and end apart: 7, of which 7 were waited for; matrix products, arithmetic and copies ran while one was open for 1% of the time, Pallas kernels for 0%

commit v1 on v0

--- a/solution.py
+++ b/solution.py
@@ -120,7 +120,9 @@
         partial_image, pullback = jax.vjp(
             lambda plane: intensity(plane, kern_real, kern_imag, tabs), tile_field
         )
-        image = lax.psum(partial_image.astype(jnp.bfloat16), "kern").astype(jnp.float32)
+        image = jnp.sum(lax.all_gather(partial_image.astype(jnp.bfloat16), "kern"), axis=0).astype(
+            jnp.float32
+        )
         resist = jax.nn.sigmoid(STEEP * (dose_now * image - 1.0))
         pressure = 2.0 * (resist - wanted) * resist * (1.0 - resist) * STEEP * dose_now
         tile_grad = pullback(pressure)[0]

time: 502 us -> 468 us (0.932)
  waiting for transfers between devices: 116 us -> 77.9 us
    psum x2 -> x0, waiting for transfers between devices: 32.6 us -> none  [per_device(): lax.psum(partial_image.astype(jnp.bfloat16), 'kern').astype(jnp.float32)]
    unnamed x6 -> x4, waiting for transfers between devices: 64.5 us -> 59.4 us
  transfers between devices with their start and end apart: 7 -> 5, of which waited for: 7 -> 5; matrix products, arithmetic and copies ran while one was open for 1% -> 1% of each run, Pallas kernels for 0% -> 0%
where the time goes in v1:
time: 468 us; the launch traced here: 463 us
  matrix products  211 us (45%)
  waiting for transfers between devices  77.9 us (17%)
  local copies, waits for them, and re-layouts  71.8 us (15%)
  blocking collectives  62 us (13%)
  between operations  15.3 us (3%)
  starting transfers between devices  13.2 us (3%)
  other arithmetic  8.44 us (2%)
    unnamed x4, waiting for transfers between devices  59.4 us
    dot_general x48, matrix products, add_kernel(): jnp.einsum('xf,tfy->txy', inv_imag, half_imag, precision=hp)  57.2 us
    dot_general x48, matrix products, add_kernel(): jnp.einsum('xf,tfy->txy', inv_real, half_real, precision=hp)  41.5 us
    all_to_all x2, blocking collectives, per_device(): lax.all_to_all(slot_grads, 'cells', split_axis=0, concat_axis=0, tiled=True)  35.6 us
    dot_general x48, matrix products, add_kernel(): jnp.einsum('xf,tfy->txy', inv_imag, half_real, precision=hp)  19.8 us
    dot_general x48, matrix products, add_kernel(): jnp.einsum('xf,tfy->txy', inv_real, half_imag, precision=hp)  19.5 us
    dynamic_update_slice x48, local copies, waits for them, and re-layouts, intensity(): result, unused = lax.scan(add_kernel, start, (kern_real, kern_imag))  18.6 us
    mul x48, local copies, waits for them, and re-layouts, add_kernel(): resp_real = pair[0] * spec_real - pair[1] * spec_imag  18.3 us
  transfers between devices with their start and end apart: 5, of which 5 were waited for; matrix products, arithmetic and copies ran while one was open for 1% of the time, Pallas kernels for 0%

profile of v1, /device:TPU:0, one launch (start us, length us, event | category | flops | bytes accessed | tf_op | source)
XLA Modules:
  0.0 463.1 jit_solution(18435872123845840357)
XLA Ops:
  9.6 6.3 %all-to-all-start = ((s32[4,1,8]{2,1,0:T(1,128)}), s32[4,1,8]{2,1,0:T(1,128)S(1)}, u32[]{:S(2)}, u32[]{:S(2)}) async-start(s32[4,1,8]{2,1,0:T(1,128)} %bitcast.3), calls=%async_computation | async-start | bytes 4096 | tf_op jit(solution)/shard_map/all_to_all | solution.py:93
  18.4 3.0 all-to-all-done
  23.7 3.4 all-to-all-start.1
  28.7 6.3 %all-to-all-done.1 = bf16[4,8,32,128]{3,2,1,0:T(8,128)(2,1)S(1)} async-done(((bf16[4,8,32,128]{3,2,1,0:T(8,128)(2,1)}), bf16[4,8,32,128]{3,2,1,0:T(8,128)(2,1)S(1)}, u32[]{:S(2)}, u32[]{:S(2)}) %all-to-all-start.1) | async-done | bytes 262176 | tf_op jit(solution)/shard_map/all_to_all | solution.py:107
  35.8 1.3 copy.116
  37.1 3.0 gather_fusion.1
  40.1 1.6 bitcast_reduce_fusion.1
  41.8 5.4 %all_gather.18 = f32[2,128,128]{2,1,0:T(8,128)S(1)} all-gather(f32[2,32,128]{2,1,0:T(8,128)S(1)} %broadcast_multiply_fusion.1), channel_id=1, replica_groups=mesh['groups'=2,'cells'=4,'corners'=2,'kern'=2] {'corners','kern'}, dimensions={1}, use_global_device_ids=true | all-gather | bytes 163840 | tf_op jit(solution)/shard_map/all_gather | solution.py:119
  49.2 1.3 broadcast.159.clone
  50.7 63.5 %while.92 = (s32[]{:T(128)}, f32[2,128,128]{1,2,0:T(8,128)S(1)}, f32[12,1,35,35]{3,2,1,0:T(8,128)S(1)}, f32[12,1,35,35]{3,2,1,0:T(8,128)S(1)}, f32[12,2,128,128]...) while((s32[]{:T(128)}, f32[2,128,128]{1,2,0:T(8,128)S(1)}, ...), condition=%wide.region_5.8_spmd.clone.clone.clone.clone, body=%wide.region_4.7_spmd.clone.clone.clone.clone.sunk | while | flops 70917336 | bytes 2121003 | solution.py:63
  114.3 2.1 all-gather
  116.7 56.9 %while.93 = (s32[]{:T(128)}, f32[2,35,35]{2,1,0:T(8,128)S(1)}, f32[2,35,35]{2,1,0:T(8,128)S(1)}, f32[12,1,35,35]{3,2,1,0:T(8,128)S(1)}, f32[12,2,128,128]{2,3,1,...) while((s32[]{:T(128)}, f32[2,35,35]{2,1,0:T(8,128)S(1)}, ...), condition=%wide.region_8.11_spmd.clone.clone.clone.clone, body=%wide.region_7.10_spmd.clone.clone.clone.clone.sunk | while | flops 70994280 | bytes 1536399 | solution.py:63
  119.1 1.3 fusion.694
  123.8 1.3 fusion.694
  128.6 1.3 fusion.694
  133.3 1.3 fusion.694
  138.0 1.3 fusion.694
  142.8 1.3 fusion.694
  147.5 1.3 fusion.694
  152.3 1.3 fusion.694
  157.0 1.3 fusion.694
  161.8 1.3 fusion.694
  166.5 1.3 fusion.694
  177.8 29.3 %all-reduce.6.cloned.1.call-done = bf16[2,128,128]{2,0,1:T(2,128)(2,1)} async-done(((bf16[2,128,128]{2,0,1:T(2,128)(2,1)}), bf16[2,128,128]{2,0,1:T(2,128)(2,1)}) %all-reduce.6.cloned.1.call-update) | async-done | bytes 65552
  208.0 1.3 copy.123
  209.3 3.0 gather_fusion.2
  212.3 1.6 copy.124
  214.4 17.8 %all_to_all.26 = f32[4,8,32,128]{3,1,2,0:T(8,128)S(1)} all-to-all(f32[4,8,32,128]{3,1,2,0:T(8,128)S(1)} %fusion.356), channel_id=1, replica_groups=mesh['groups'=2,'cells'=4,'corners'=2,'kern'=2] {'cells'}, dimensions={0} | all-to-all | bytes 1048576 | tf_op jit(solution)/shard_map/all_to_all | solution.py:138
  232.6 5.7 %psum.14 = f32[8]{0:T(128)S(1)} all-reduce(f32[8]{0:T(128)S(1)} %get-tuple-element.1427), channel_id=1, replica_groups=mesh['groups'=2,'cells'=4,'corners'=2,'kern'=2] {'corners','kern'}, use_global_device_ids=true, to_apply=%region_11.14 | all-reduce | flops 8 | bytes 64 | tf_op jit(solution)/shard_map/psum | solution.py:144
  240.1 3.4 all-to-all-start.3
  243.6 9.1 %all-to-all-done.3 = bf16[4,8,32,128]{3,2,1,0:T(8,128)(2,1)S(1)} async-done(((bf16[4,8,32,128]{3,2,1,0:T(8,128)(2,1)}), bf16[4,8,32,128]{3,2,1,0:T(8,128)(2,1)S(1)}, u32[]{:S(2)}, u32[]{:S(2)}) %all-to-all-start.3) | async-done | bytes 262176 | tf_op jit(solution)/shard_map/all_to_all | solution.py:107
  253.4 1.3 copy.128
  254.7 3.0 gather_fusion.4
  257.7 1.6 bitcast_reduce_fusion
  259.4 5.6 %all_gather.21 = f32[2,128,128]{2,1,0:T(8,128)S(1)} all-gather(f32[2,32,128]{2,1,0:T(8,128)S(1)} %broadcast_multiply_fusion), channel_id=1, replica_groups=mesh['groups'=2,'cells'=4,'corners'=2,'kern'=2] {'corners','kern'}, dimensions={1}, use_global_device_ids=true | all-gather | bytes 163840 | tf_op jit(solution)/shard_map/all_gather | solution.py:119
  267.0 1.3 broadcast.159
  268.6 63.5 %while.94 = (s32[]{:T(128)}, f32[2,128,128]{1,2,0:T(8,128)S(1)}, f32[12,1,35,35]{3,2,1,0:T(8,128)S(1)}, f32[12,1,35,35]{3,2,1,0:T(8,128)S(1)}, f32[12,2,128,128]...) while((s32[]{:T(128)}, f32[2,128,128]{1,2,0:T(8,128)S(1)}, ...), condition=%wide.region_14.17_spmd.clone.clone.clone.clone, body=%wide.region_13.16_spmd.clone.clone.clone.clone.sunk | while | flops 70917336 | bytes 2121003 | solution.py:63
  332.2 1.9 all-gather.1
  334.3 56.9 %while.95 = (s32[]{:T(128)}, f32[2,35,35]{2,1,0:T(8,128)S(1)}, f32[2,35,35]{2,1,0:T(8,128)S(1)}, f32[12,1,35,35]{3,2,1,0:T(8,128)S(1)}, f32[12,2,128,128]{2,3,1,...) while((s32[]{:T(128)}, f32[2,35,35]{2,1,0:T(8,128)S(1)}, ...), condition=%wide.region_17.20_spmd.clone.clone.clone.clone, body=%wide.region_16.19_spmd.clone.clone.clone.clone.sunk | while | flops 70994280 | bytes 1536399 | solution.py:63
  336.7 1.3 fusion.731
  360.4 1.3 fusion.731
  374.7 1.3 fusion.731
  394.2 30.1 %all-reduce.8.cloned.1.call-done = bf16[2,128,128]{2,0,1:T(2,128)(2,1)} async-done(((bf16[2,128,128]{2,0,1:T(2,128)(2,1)}), bf16[2,128,128]{2,0,1:T(2,128)(2,1)}) %all-reduce.8.cloned.1.call-update) | async-done | bytes 65552
  425.1 1.3 copy.134
  426.4 3.0 gather_fusion.5
  429.4 1.6 copy.135
  431.5 17.8 %all_to_all.27 = f32[4,8,32,128]{3,1,2,0:T(8,128)S(1)} all-to-all(f32[4,8,32,128]{3,1,2,0:T(8,128)S(1)} %fusion.354), channel_id=1, replica_groups=mesh['groups'=2,'cells'=4,'corners'=2,'kern'=2] {'cells'}, dimensions={0} | all-to-all | bytes 1048576 | tf_op jit(solution)/shard_map/all_to_all | solution.py:138
  449.8 5.7 %psum.15 = f32[8]{0:T(128)S(1)} all-reduce(f32[8]{0:T(128)S(1)} %get-tuple-element.1429), channel_id=1, replica_groups=mesh['groups'=2,'cells'=4,'corners'=2,'kern'=2] {'corners','kern'}, use_global_device_ids=true, to_apply=%region_20.23 | all-reduce | flops 8 | bytes 64 | tf_op jit(solution)/shard_map/psum | solution.py:144
  (577 shorter events, 246.4 us)
Async XLA Ops:
  6.5 11.9 %copy-start = (f32[8,128,128]{2,1,0:T(8,128)S(1)}, f32[8,128,128]{2,1,0:T(8,128)}, u32[]{:S(2)}) copy-start(f32[8,128,128]{2,1,0:T(8,128)} %param.19) | copy-start | bytes 1572868
  9.6 11.8 %all-to-all-start = ((s32[4,1,8]{2,1,0:T(1,128)}), s32[4,1,8]{2,1,0:T(1,128)S(1)}, u32[]{:S(2)}, u32[]{:S(2)}) async-start(s32[4,1,8]{2,1,0:T(1,128)} %bitcast.3), calls=%async_computation | async-start | bytes 4096 | tf_op jit(solution)/shard_map/all_to_all | solution.py:93
  23.7 11.3 %all-to-all-start.1 = ((bf16[4,8,32,128]{3,2,1,0:T(8,128)(2,1)}), bf16[4,8,32,128]{3,2,1,0:T(8,128)(2,1)S(1)}, u32[]{:S(2)}, u32[]{:S(2)}) async-start(bf16[4,8,32,128]{3,2,1,0:T(8,128)(2,1)} %copy.115), calls=%async_computation.1 | async-start | bytes 524288 | tf_op jit(solution)/shard_map/all_to_all | solution.py:107
  27.2 180.0 %all-reduce.6.cloned.1.call-start = ((), (), s32[]{:S(2)}) async-start(), calls=%async_computation.5 | async-start | bytes 131072
  50.7 65.7 %copy-start.3 = (bf16[2,128,128]{2,1,0:T(8,128)(2,1)S(1)}, bf16[2,128,128]{2,1,0:T(8,128)(2,1)}, u32[]{:S(2)}) copy-start(bf16[2,128,128]{2,1,0:T(8,128)(2,1)} %param.20) | copy-start | bytes 196612
  116.7 59.9 %copy-start.5 = (u32[32]{0:T(128)S(1)}, u32[32]{0:T(128)}, u32[]{:S(2)}) copy-start(u32[32]{0:T(128)} %constant.356) | copy-start | bytes 388
  238.4 0.7 copy-start.1
  240.1 12.6 %all-to-all-start.3 = ((bf16[4,8,32,128]{3,2,1,0:T(8,128)(2,1)}), bf16[4,8,32,128]{3,2,1,0:T(8,128)(2,1)S(1)}, u32[]{:S(2)}, u32[]{:S(2)}) async-start(bf16[4,8,32,128]{3,2,1,0:T(8,128)(2,1)} %copy.127), calls=%async_computation.3 | async-start | bytes 524288 | tf_op jit(solution)/shard_map/all_to_all | solution.py:107
  243.5 180.8 %all-reduce.8.cloned.1.call-start = ((), (), s32[]{:S(2)}) async-start(), calls=%async_computation.6 | async-start | bytes 131072
  268.6 65.5 %copy-start.4 = (bf16[2,128,128]{2,1,0:T(8,128)(2,1)S(1)}, bf16[2,128,128]{2,1,0:T(8,128)(2,1)}, u32[]{:S(2)}) copy-start(bf16[2,128,128]{2,1,0:T(8,128)(2,1)} %param.20) | copy-start | bytes 196612
  429.4 19.9 %copy-start.2 = (f32[8,32,128]{2,0,1:T(8,128)S(1)}, f32[8,32,128]{2,0,1:T(8,128)}, u32[]{:S(2)}) copy-start(f32[8,32,128]{2,0,1:T(8,128)} %copy-done.1) | copy-start | bytes 393220
Sparse Core Ops, SparseCore 0:
  176.7 30.4 all-reduce.5
  394.3 29.8 all-reduce.7
